TPU v7x, 32 devices: a whole 2x2x4 slice. The times are simulated.
32 devices in a mesh: group: 4 (over y, x), patch: 8 (over z, core).
Axes of the slice: x: 2, y: 2, z: 4, core: 2. Of those that a mesh axis runs over, the one named last changes fastest.
Arguments:
- node_tape: bfloat16 [4, 8192, 512], P('group', 'patch'), may hold values from -6 to 6
- edge_tape: bfloat16 [4, 8192, 512], P('group', 'patch'), may hold values from -6 to 6
- node_cot: bfloat16 [4, 8192, 512], P('group', 'patch'), may hold values from -6 to 6
- edge_cot: bfloat16 [4, 8192, 512], P('group', 'patch'), may hold values from -6 to 6
- w_edge_in: bfloat16 [1536, 512], replicated, may hold values from -0.15625 to 0.15625
- w_edge_out: bfloat16 [512, 512], replicated, may hold values from -0.25 to 0.25
- gain_edge: float32 [512], replicated, may hold values from 0.1 to 1.9
- w_node_in: bfloat16 [1024, 512], replicated, may hold values from -0.1875 to 0.1875
- w_node_out: bfloat16 [512, 512], replicated, may hold values from -0.25 to 0.25
- gain_node: float32 [512], replicated, may hold values from 0.1 to 1.9
- senders: int32 [64, 128], P('patch'), may hold values from 0 to 1279
- receivers: int32 [64, 128], P('patch'), may hold values from 0 to 1023
- tile_count: int32 [8], P('patch'), may hold values from 1 to 8, as said below
- send_rows: int32 [8, 256], P('patch'), may hold values from 0 to 1023
Outputs:
- edge_grad: bfloat16 [4, 8192, 512], P('group', 'patch')
- node_grad: bfloat16 [4, 8192, 512], P('group', 'patch')
- grad_edge_in: float32 [1536, 512], P('patch')
- grad_edge_out: float32 [512, 512], P('patch')
- grad_gain_edge: float32 [512], P('patch')
- grad_node_in: float32 [1024, 512], P('patch')
- grad_node_out: float32 [512, 512], P('patch')
- grad_gain_node: float32 [512], P('patch')
Inputs may be any that keep to these rules, and one draw needn't show every extreme that they name: Tiles 0 to tile_count - 1 of a patch's 8 slots hold edges, the rest are padding; some patch has all 8 live. `senders`: A value s below 1024 is a node of the edge's own patch; 1024 + k is the k-th halo row that patch receives, rows p * 32 to (p + 1) * 32 - 1 coming from patch p. `receivers`: A node of the edge's own patch. `send_rows`: entry p * 32 + j of patch q's list is the own node whose latent is the j-th halo row patch p receives from q; every patch sends exactly 32 rows to every patch.
All inputs are finite; a program needn't handle non-finite values.
Results may differ from a plain program's by a relative error of at most 0.014.
Values may be sent and summed in bfloat16 or wider, within the bound.
A program may use at most 128 MiB of HBM per device.

v0:
```python
import jax
import jax.numpy as jnp
from jax import lax
from jax.sharding import PartitionSpec as P

epsilon = 1e-05


def product(left, right):
    return jnp.dot(left, right, preferred_element_type=jnp.float32)


def silu_slope(values):
    squash = jax.nn.sigmoid(values)
    return squash * (1.0 + values * (1.0 - squash))


def normalize(values):
    centred = values - jnp.mean(values, axis=1, keepdims=True)
    inverse = lax.rsqrt(jnp.mean(centred * centred, axis=1, keepdims=True) + epsilon)
    return (centred * inverse, inverse)


def normalize_back(upstream, normed, inverse):
    return inverse * (
        upstream
        - jnp.mean(upstream, axis=1, keepdims=True)
        - normed * jnp.mean(upstream * normed, axis=1, keepdims=True)
    )


def local(
    node_tape,
    edge_tape,
    node_cot,
    edge_cot,
    w_edge_in,
    w_edge_out,
    gain_edge,
    w_node_in,
    w_node_out,
    gain_node,
    senders,
    receivers,
    tile_count,
    send_rows,
):
    node_rows = node_tape[0]
    edge_rows = edge_tape[0]
    features = node_rows.shape[1]
    node_count = node_rows.shape[0]
    outgoing = jnp.take(node_rows, send_rows[0], axis=0)
    incoming = lax.all_to_all(outgoing, "patch", split_axis=0, concat_axis=0, tiled=True)
    extended = jnp.concatenate([node_rows, incoming], axis=0)
    send_index = senders.reshape(-1)
    recv_index = receivers.reshape(-1)
    send_latent = jnp.take(extended, send_index, axis=0)
    recv_latent = jnp.take(node_rows, recv_index, axis=0)
    tile_slot = jnp.arange(edge_rows.shape[0], dtype=jnp.int32) // senders.shape[1]
    live_mask = (tile_slot < tile_count[0]).astype(jnp.float32)[:, None]
    edge_input = jnp.concatenate([edge_rows, send_latent, recv_latent], axis=1)
    edge_first = product(edge_input, w_edge_in)
    hidden = jax.nn.silu(edge_first).astype(jnp.bfloat16)
    second = product(hidden, w_edge_out)
    normed_edge, inverse_edge = normalize(second)
    message = live_mask * (gain_edge * normed_edge)
    gathered = jax.ops.segment_sum(message, recv_index, num_segments=node_count).astype(
        jnp.bfloat16
    )
    joined = jnp.concatenate([node_rows, gathered], axis=1)
    node_first = product(joined, w_node_in)
    node_hidden = jax.nn.silu(node_first).astype(jnp.bfloat16)
    node_second = product(node_hidden, w_node_out)
    normed_node, inverse_node = normalize(node_second)
    node_upstream = node_cot[0].astype(jnp.float32)
    part_gain_node = jnp.sum(node_upstream * normed_node, axis=0)
    grad_second = normalize_back(node_upstream * gain_node, normed_node, inverse_node).astype(
        jnp.bfloat16
    )
    part_node_out = product(node_hidden.T, grad_second)
    grad_first = (product(grad_second, w_node_out.T) * silu_slope(node_first)).astype(jnp.bfloat16)
    part_node_in = product(joined.T, grad_first)
    grad_joined = product(grad_first, w_node_in.T)
    edge_back = edge_cot[0].astype(jnp.float32)
    grad_message = live_mask * (edge_back + jnp.take(grad_joined[:, features:], recv_index, axis=0))
    part_gain_edge = jnp.sum(grad_message * normed_edge, axis=0)
    grad_edge_second = normalize_back(grad_message * gain_edge, normed_edge, inverse_edge).astype(
        jnp.bfloat16
    )
    part_edge_out = product(hidden.T, grad_edge_second)
    grad_edge_first = (product(grad_edge_second, w_edge_out.T) * silu_slope(edge_first)).astype(
        jnp.bfloat16
    )
    part_edge_in = product(edge_input.T, grad_edge_first)
    grad_input = product(grad_edge_first, w_edge_in.T)
    edge_grad = (live_mask * edge_back + grad_input[:, :features]).astype(jnp.bfloat16)
    spread = jax.ops.segment_sum(
        grad_input[:, features : 2 * features], send_index, num_segments=extended.shape[0]
    )
    returned = lax.all_to_all(
        spread[node_count:].astype(jnp.bfloat16), "patch", split_axis=0, concat_axis=0, tiled=True
    ).astype(jnp.float32)
    from_recv = jax.ops.segment_sum(
        grad_input[:, 2 * features :], recv_index, num_segments=node_count
    )
    from_halo = jax.ops.segment_sum(returned, send_rows[0], num_segments=node_count)
    node_grad = (
        node_upstream + grad_joined[:, :features] + spread[:node_count] + from_recv + from_halo
    ).astype(jnp.bfloat16)
    partials = (
        part_edge_in,
        part_edge_out,
        part_gain_edge,
        part_node_in,
        part_node_out,
        part_gain_node,
    )
    pieces = (
        lax.psum_scatter(partials[0], "patch", scatter_dimension=0, tiled=True),
        lax.psum_scatter(partials[1], "patch", scatter_dimension=0, tiled=True),
        lax.psum_scatter(partials[2], "patch", scatter_dimension=0, tiled=True),
        lax.psum_scatter(partials[3], "patch", scatter_dimension=0, tiled=True),
        lax.psum_scatter(partials[4], "patch", scatter_dimension=0, tiled=True),
        lax.psum_scatter(partials[5], "patch", scatter_dimension=0, tiled=True),
    )
    shares = (
        lax.psum(pieces[0].astype(jnp.bfloat16), "group").astype(jnp.float32),
        lax.psum(pieces[1].astype(jnp.bfloat16), "group").astype(jnp.float32),
        lax.psum(pieces[2].astype(jnp.bfloat16), "group").astype(jnp.float32),
        lax.psum(pieces[3].astype(jnp.bfloat16), "group").astype(jnp.float32),
        lax.psum(pieces[4].astype(jnp.bfloat16), "group").astype(jnp.float32),
        lax.psum(pieces[5].astype(jnp.bfloat16), "group").astype(jnp.float32),
    )
    factor = float(lax.axis_size("group") * lax.axis_size("patch") * edge_rows.shape[0]) ** (-0.5)
    return (
        edge_grad[None],
        node_grad[None],
        shares[0] * factor,
        shares[1] * factor,
        shares[2] * factor,
        shares[3] * factor,
        shares[4] * factor,
        shares[5] * factor,
    )


def solution(mesh):
    placed = (
        P("group", "patch", None),
        P("group", "patch", None),
        P("group", "patch", None),
        P("group", "patch", None),
        P(),
        P(),
        P(),
        P(),
        P(),
        P(),
        P("patch", None),
        P("patch", None),
        P("patch"),
        P("patch", None),
    )
    return jax.shard_map(
        local,
        mesh=mesh,
        in_specs=placed,
        out_specs=(
            P("group", "patch", None),
            P("group", "patch", None),
            P("patch", None),
            P("patch", None),
            P("patch"),
            P("patch", None),
            P("patch", None),
            P("patch"),
        ),
        check_vma=False,
    )
```

profile of v0, /device:TPU:0, one launch (start us, length us, event | category | flops | bytes accessed | tf_op | source)
XLA Modules:
  0.0 289.5 jit_solution(9949390608979094338)
XLA Ops:
  9.9 2.6 gather_fusion
  13.3 6.4 %all-to-all-start = ((bf16[8,32,512]{2,1,0:T(8,128)(2,1)}), bf16[8,32,512]{2,1,0:T(8,128)(2,1)S(1)}, u32[]{:S(2)}, u32[]{:S(2)}) async-start(bf16[8,32,512]{2,1,0:T(8,128)(2,1)} %broadcast_select_fusion.2), calls=%async_computation | async-start | bytes 524288 | tf_op jit(solution)/shard_map/all_to_all | solution.py:53
  25.1 5.1 %gather_fusion.2 = bf16[1024,512]{1,0:T(8,128)(2,1)} fusion(bf16[1024,512]{1,0:T(8,128)(2,1)S(1)} %bitcast.66, s32[1024]{0:T(1024)S(1)} %broadcast_clamp_fusion.1), kind=kCustom, calls=%fused_computation.2 | custom fusion | bytes 2101248 | tf_op jit(solution)/shard_map/jit(_take)/gather | solution.py:58
  35.9 6.6 %gather_fusion.1 = bf16[1024,512]{1,0:T(8,128)(2,1)} fusion(bf16[1280,512]{1,0:T(8,128)(2,1)} %pad_maximum_fusion.4, s32[1024]{0:T(1024)S(1)} %broadcast_clamp_fusion), kind=kCustom, calls=%fused_computation.1 | custom fusion | bytes 2101248 | tf_op jit(solution)/shard_map/jit(_take)/gather | solution.py:57
  46.7 3.3 %multiply_convert_fusion.4 = (bf16[1024,512]{1,0:T(8,128)(2,1)S(1)}, f32[1024,512]{1,0:T(8,128)}) fusion(bf16[1536,512]{1,0:T(8,128)(2,1)S(1)} %copy-done, bf16[1024,512]{0,1:T(8,128)(2,1)S(1)} %get-tuple-element.56, bf16[1024,512]{0,1:T(8,128)(2,1)S(1)} %get-tuple-element.57, bf16[1024,512]{0,1:T(8,128)(2,1)S(1)} %bitcast.73), kind=kOutput, calls=%fused_computation.42 | convolution fusion | flops 1622671360 | bytes 7864320 | tf_op jit(solution)/shard_map/dot_general | solution.py:10
  53.7 3.0 %copy.55 = f32[1024,512]{1,0:T(8,128)} copy(f32[1024,512]{0,1:T(8,128)} %multiply_multiply_fusion) | data formatting | bytes 4194304 | tf_op jit(solution)/shard_map/mul | solution.py:66
  56.7 8.6 %scatter_custom_fusion = f32[1024,512]{1,0:T(8,128)} fusion(s32[1024]{0:T(1024)S(1)} %bitcast.78, f32[1024,512]{1,0:T(8,128)} %copy.55, f32[]{:T(128)} %constant.93.clone.1), kind=kCustom, calls=%fused_computation.57 | custom fusion | flops 524288 | bytes 2097664 | tf_op jit(solution)/shard_map/scatter-add | solution.py:67
  67.2 2.8 multiply_convert_fusion.3
  75.5 4.1 %multiply_convert_fusion.2 = bf16[1024,512]{1,0:T(8,128)(2,1)} fusion(f32[1024,512]{1,0:T(8,128)} %get-tuple-element.53, bf16[1024,512]{0,1:T(8,128)(2,1)} %copy-done.22, bf16[512,512]{1,0:T(8,128)(2,1)S(1)} %copy-done.23), kind=kOutput, calls=%fused_computation.36 | convolution fusion | flops 541589504 | bytes 4718592 | tf_op jit(solution)/shard_map/dot_general | solution.py:10
  79.6 2.8 fusion.40
  85.0 6.8 %gather_fusion.3 = f32[1024,512]{1,0:T(8,128)} fusion(f32[1024,512]{1,0:T(8,128)} %get-tuple-element.47, s32[1024]{0:T(1024)S(1)} %broadcast_clamp_fusion.1), kind=kCustom, calls=%fused_computation.3 | custom fusion | bytes 4198400 | tf_op jit(solution)/shard_map/jit(_take)/gather | solution.py:85
  91.8 2.9 %copy.57 = f32[1024,512]{0,1:T(8,128)} copy(f32[1024,512]{1,0:T(8,128)} %gather_fusion.3) | data formatting | bytes 4194304 | tf_op jit(solution)/shard_map/jit(_take)/gather | solution.py:85
  94.7 3.6 %multiply_reduce_fusion = (f32[512]{0:T(512)S(1)}, f32[1024]{0:T(1024)S(1)}, f32[1024]{0:T(1024)S(1)}) fusion(f32[1024,512]{0,1:T(8,128)} %copy-done.2, f32[1024]{0:T(1024)S(1)} %add_rsqrt_fusion.1, f32[1024]{0:T(1024)S(1)} %broadcast_multiply_fusion.5, f32[1024,512]{0,1:T(8,128)} %copy.57, pred[1024]{0:T(1024)(128)(4,1)S(1)} %compare_and_fusion, ...), kind=kLoop, calls=%fused_computation.31 | loop fusion | flops 6288896 | bytes 5268480 | tf_op jit(solution)/shard_map/reduce_sum | solution.py:86
  102.4 4.1 %fusion.16 = f32[1024,512]{1,0:T(8,128)} fusion(bf16[1024,512]{1,0:T(8,128)(2,1)} %multiply_convert_fusion.2, bf16[1024,512]{1,0:T(8,128)(2,1)} %copy-done.11, bf16[1024,512]{1,0:T(8,128)(2,1)S(1)} %bitcast.69), kind=kOutput, calls=%fused_computation.47 | convolution fusion | flops 1077936128 | bytes 5242880 | tf_op jit(solution)/shard_map/dot_general | solution.py:10
  108.0 3.0 %multiply_convert_fusion = bf16[1024,512]{1,0:T(8,128)(2,1)S(1)} fusion(f32[1024,512]{1,0:T(8,128)} %get-tuple-element.49, bf16[1024,512]{0,1:T(8,128)(2,1)S(1)} %copy-done.21, bf16[512,512]{1,0:T(8,128)(2,1)S(1)} %copy-done.25), kind=kOutput, calls=%fused_computation.33 | convolution fusion | flops 541589504 | bytes 4718592 | tf_op jit(solution)/shard_map/dot_general | solution.py:10
  111.9 3.5 %fusion.19 = f32[1536,512]{1,0:T(8,128)} fusion(bf16[1024,512]{1,0:T(8,128)(2,1)S(1)} %multiply_convert_fusion, bf16[1024,512]{0,1:T(8,128)(2,1)S(1)} %copy-done.15, bf16[1024,512]{0,1:T(8,128)(2,1)S(1)} %copy-done.17, bf16[1024,512]{0,1:T(8,128)(2,1)S(1)} %bitcast.74), kind=kOutput, calls=%fused_computation.51 | convolution fusion | flops 1620049920 | bytes 7340032 | tf_op jit(solution)/shard_map/dot_general | solution.py:10
  119.1 2.7 copy-done.10
  123.3 9.0 %scatter_custom_fusion.1 = f32[1280,512]{1,0:T(8,128)} fusion(s32[1024]{0:T(1024)S(1)} %bitcast.76, f32[1024,1536]{1,0:T(8,128)} %copy-done.10, f32[]{:T(128)} %constant.93.clone.1), kind=kCustom, calls=%fused_computation.28 | custom fusion | flops 524288 | bytes 4719104 | tf_op jit(solution)/shard_map/scatter-add | solution.py:97
  134.0 3.2 %slice.41 = f32[1024,512]{1,0:T(8,128)} slice(f32[1280,512]{1,0:T(8,128)} %scatter_custom_fusion.1), slice={[0:1024], [0:512]} | slice | bytes 4194304 | tf_op jit(solution)/shard_map/slice | solution.py:108
  137.2 2.9 %copy.64 = f32[1024,512]{0,1:T(8,128)} copy(f32[1024,512]{1,0:T(8,128)} %get-tuple-element.46) | data formatting | bytes 4194304
  140.1 2.9 copy.63
  143.0 3.0 %copy.65 = f32[1024,512]{0,1:T(8,128)} copy(f32[1024,512]{1,0:T(8,128)} %slice.41) | data formatting | bytes 4194304
  146.0 5.1 %all-to-all-start.1 = ((bf16[8,32,512]{2,1,0:T(8,128)(2,1)}), bf16[8,32,512]{2,1,0:T(8,128)(2,1)S(1)}, u32[]{:S(2)}, u32[]{:S(2)}) async-start(bf16[8,32,512]{2,1,0:T(8,128)(2,1)} %bitcast.19), calls=%async_computation.1 | async-start | bytes 524288 | tf_op jit(solution)/shard_map/all_to_all | solution.py:100
  151.2 4.6 %fusion.10 = f32[1024,512]{0,1:T(8,128)} fusion(f32[1024,512]{0,1:T(8,128)} %copy.65, f32[1024,512]{0,1:T(8,128)} %copy.64, bf16[1,1024,512]{1,2,0:T(8,128)(2,1)S(1)} %copy-done.6), kind=kLoop, calls=%fused_computation.24 | loop fusion | flops 1572864 | bytes 7340032 | tf_op jit(solution)/shard_map/add | solution.py:108
  156.2 17.2 %all-reduce.2 = (bf16[512]{0:T(512)(128)(2,1)S(1)}, bf16[512]{0:T(512)(128)(2,1)S(1)}) all-reduce(f32[512]{0:T(512)S(1)} %get-tuple-element.32, f32[512]{0:T(512)S(1)} %get-tuple-element.34), channel_id=4, replica_groups=mesh['group'=4,'patch'=8] {'patch'}, use_global_device_ids=true, to_apply=%region_17.18.clone | all-reduce | flops 1024 | bytes 6144
  173.5 10.2 %all-reduce.3 = (bf16[64]{0:T(256)(128)(2,1)S(1)}, bf16[64]{0:T(256)(128)(2,1)S(1)}) all-reduce(bf16[64]{0:T(256)(128)(2,1)S(1)} %dynamic-slice.7, bf16[64]{0:T(256)(128)(2,1)S(1)} %dynamic-slice.6), channel_id=1, replica_groups=mesh['group'=4,'patch'=8] {'group'}, use_global_device_ids=true, to_apply=%region_18.19 | all-reduce | flops 128 | bytes 512 | tf_op jit(solution)/shard_map/psum | solution.py:129
  188.9 39.4 %reduce-scatter.5.cloned.1.call-done = f32[192,512]{1,0:T(8,128)} async-done(((f32[1536,512]{1,0:T(8,128)}), f32[192,512]{1,0:T(8,128)}) %reduce-scatter.5.cloned.1.call-update) | async-done | bytes 393232 | tf_op jit(solution)/shard_map/reduce_scatter | solution.py:119
  231.8 2.9 %copy.61 = f32[1024,512]{1,0:T(8,128)} copy(f32[1024,512]{0,1:T(8,128)} %fusion.10) | data formatting | bytes 4194304 | tf_op jit(solution)/shard_map/add | solution.py:108
  234.7 10.3 %scatter_custom_fusion.2 = f32[1024,512]{1,0:T(8,128)} fusion(f32[1024,512]{1,0:T(8,128)} %copy.61, s32[1024]{0:T(1024)S(1)} %bitcast.79, f32[1024,1536]{1,0:T(8,128)} %copy-done.10), kind=kCustom, calls=%fused_computation.26 | custom fusion | flops 524288 | bytes 4194304 | tf_op jit(solution)/shard_map/scatter-add | solution.py:103
  245.1 3.6 %scatter_custom_fusion.3 = f32[1024,512]{1,0:T(8,128)} fusion(s32[256]{0:T(256)} %bitcast.83, f32[]{:T(128)} %constant.93.clone.1, bf16[256,512]{1,0:T(8,128)(2,1)S(1)} %bitcast.70), kind=kCustom, calls=%fused_computation.55 | custom fusion | flops 262144 | bytes 2359808 | tf_op jit(solution)/shard_map/scatter-add | solution.py:106
  248.7 3.5 %fusion.21 = bf16[1,1024,512]{2,1,0:T(8,128)(2,1)} fusion(f32[1024,512]{1,0:T(8,128)} %scatter_custom_fusion.2, f32[1024,512]{1,0:T(8,128)} %scatter_custom_fusion.3), kind=kLoop, calls=%fused_computation.53 | loop fusion | flops 1048576 | bytes 5242880 | tf_op jit(solution)/shard_map/broadcast_in_dim | solution.py:137
  252.2 24.3 %all-reduce.7.cloned.1.call-done = (bf16[192,512]{1,0:T(8,128)(2,1)}, bf16[64,512]{1,0:T(8,128)(2,1)}, bf16[128,512]{1,0:T(8,128)(2,1)}, bf16[64,512]{1,0:T(8,128)(2,1)}) async-done(((bf16[192,512]{1,0:T(8,128)(2,1)}, bf16[64,512]{1,0:T(8,128)(2,1)}, bf16[128,512]{1,0:T(8,128)(2,1)}, bf16[64,512]{1,0:T(8,128)(2,1)}), (bf16[192,512]{1,0:T(8,128)(2,1)}, bf16[64,512]{1,0:T(8,128)(2,1)}, ...) | async-done | bytes 458768 | tf_op jit(solution)/shard_map/psum | solution.py:127
  (141 shorter events, 60.1 us)
Async XLA Ops:
  7.2 39.5 %copy-start = (bf16[1536,512]{1,0:T(8,128)(2,1)S(1)}, bf16[1536,512]{1,0:T(8,128)(2,1)}, u32[]{:S(2)}) copy-start(bf16[1536,512]{1,0:T(8,128)(2,1)} %param.18) | copy-start | bytes 4718596
  7.2 13.2 %copy-start.28 = (s32[8,128]{1,0:T(8,128)S(1)}, s32[8,128]{1,0:T(8,128)}, u32[]{:S(2)}) copy-start(s32[8,128]{1,0:T(8,128)} %param.25) | copy-start | bytes 12292
  7.2 13.2 %copy-start.27 = (s32[8,128]{1,0:T(8,128)S(1)}, s32[8,128]{1,0:T(8,128)}, u32[]{:S(2)}) copy-start(s32[8,128]{1,0:T(8,128)} %param.24) | copy-start | bytes 12292
  13.3 21.4 %all-to-all-start = ((bf16[8,32,512]{2,1,0:T(8,128)(2,1)}), bf16[8,32,512]{2,1,0:T(8,128)(2,1)S(1)}, u32[]{:S(2)}, u32[]{:S(2)}) async-start(bf16[8,32,512]{2,1,0:T(8,128)(2,1)} %broadcast_select_fusion.2), calls=%async_computation | async-start | bytes 524288 | tf_op jit(solution)/shard_map/all_to_all | solution.py:53
  19.7 164.5 %reduce-scatter.11.cloned.1.call-start = ((), (), s32[]{:S(2)}) async-start(), calls=%async_computation.9 | async-start | bytes 1179648 | tf_op jit(solution)/shard_map/reduce_scatter | solution.py:123
  20.5 4.7 %copy-start.1 = (bf16[1,1024,512]{2,1,0:T(8,128)(2,1)S(1)}, bf16[1,1024,512]{2,1,0:T(8,128)(2,1)}, u32[]{:S(2)}) copy-start(bf16[1,1024,512]{2,1,0:T(8,128)(2,1)} %param.14) | copy-start | bytes 3145732
  44.8 1.9 copy-start.12
  46.6 3.4 %copy-start.14 = (bf16[1024,512]{0,1:T(8,128)(2,1)}, bf16[1024,512]{0,1:T(8,128)(2,1)S(1)}, u32[]{:S(2)}) copy-start(bf16[1024,512]{0,1:T(8,128)(2,1)S(1)} %get-tuple-element.56) | copy-start | bytes 3145732
  46.6 3.4 %copy-start.16 = (bf16[1024,512]{0,1:T(8,128)(2,1)}, bf16[1024,512]{0,1:T(8,128)(2,1)S(1)}, u32[]{:S(2)}) copy-start(bf16[1024,512]{0,1:T(8,128)(2,1)S(1)} %get-tuple-element.57) | copy-start | bytes 3145732
  46.7 3.3 %copy-start.24 = (bf16[512,512]{1,0:T(8,128)(2,1)S(1)}, bf16[512,512]{1,0:T(8,128)(2,1)}, u32[]{:S(2)}) copy-start(bf16[512,512]{1,0:T(8,128)(2,1)} %param.19) | copy-start | bytes 1572868
  50.0 2.1 copy-start.26
  65.4 1.9 copy-start.30
  67.2 2.8 copy-start.11
  67.2 2.8 copy-start.23
  79.6 106.2 %reduce-scatter.7.cloned.1.call-start = ((), (), s32[]{:S(2)}) async-start(), calls=%async_computation.7 | async-start | bytes 1179648 | tf_op jit(solution)/shard_map/reduce_scatter | solution.py:120
  94.7 3.6 %copy-start.3 = (f32[1024,512]{0,1:T(8,128)S(1)}, f32[1024,512]{0,1:T(8,128)}, u32[]{:S(2)}) copy-start(f32[1024,512]{0,1:T(8,128)} %copy-done.2) | copy-start | bytes 6291460
  94.7 3.8 %copy-start.4 = (f32[1024,512]{0,1:T(8,128)S(1)}, f32[1024,512]{0,1:T(8,128)}, u32[]{:S(2)}) copy-start(f32[1024,512]{0,1:T(8,128)} %copy.57) | copy-start | bytes 6291460
  94.7 4.1 %copy-start.7 = (bf16[1,1024,512]{1,2,0:T(8,128)(2,1)S(1)}, bf16[1,1024,512]{1,2,0:T(8,128)(2,1)}, u32[]{:S(2)}) copy-start(bf16[1,1024,512]{1,2,0:T(8,128)(2,1)} %copy.51) | copy-start | bytes 3145732
  98.8 1.8 copy-start.19
  102.4 84.9 %reduce-scatter.9.cloned.1.call-start = ((), (), s32[]{:S(2)}) async-start(), calls=%async_computation.8 | async-start | bytes 2359296 | tf_op jit(solution)/shard_map/reduce_scatter | solution.py:122
  106.6 1.4 copy-start.25
  106.6 121.7 %reduce-scatter.5.cloned.1.call-start = ((), (), s32[]{:S(2)}) async-start(), calls=%async_computation.6 | async-start | bytes 3538944 | tf_op jit(solution)/shard_map/reduce_scatter | solution.py:119
  107.9 3.9 %copy-start.13 = (bf16[1,1024,512]{1,2,0:T(8,128)(2,1)S(1)}, bf16[1,1024,512]{1,2,0:T(8,128)(2,1)}, u32[]{:S(2)}) copy-start(bf16[1,1024,512]{1,2,0:T(8,128)(2,1)} %copy.52) | copy-start | bytes 3145732
  108.0 3.9 %copy-start.15 = (bf16[1024,512]{0,1:T(8,128)(2,1)S(1)}, bf16[1024,512]{0,1:T(8,128)(2,1)}, u32[]{:S(2)}) copy-start(bf16[1024,512]{0,1:T(8,128)(2,1)} %copy-done.14) | copy-start | bytes 3145732
  108.0 3.9 %copy-start.17 = (bf16[1024,512]{0,1:T(8,128)(2,1)S(1)}, bf16[1024,512]{0,1:T(8,128)(2,1)}, u32[]{:S(2)}) copy-start(bf16[1024,512]{0,1:T(8,128)(2,1)} %copy-done.16) | copy-start | bytes 3145732
  115.4 1.9 copy-start.33
  119.1 2.7 copy-start.10
  143.0 8.2 %copy-start.6 = (bf16[1,1024,512]{1,2,0:T(8,128)(2,1)S(1)}, bf16[1,1024,512]{1,2,0:T(8,128)(2,1)}, u32[]{:S(2)}) copy-start(bf16[1,1024,512]{1,2,0:T(8,128)(2,1)} %copy.56) | copy-start | bytes 3145732
  146.0 99.1 %all-to-all-start.1 = ((bf16[8,32,512]{2,1,0:T(8,128)(2,1)}), bf16[8,32,512]{2,1,0:T(8,128)(2,1)S(1)}, u32[]{:S(2)}, u32[]{:S(2)}) async-start(bf16[8,32,512]{2,1,0:T(8,128)(2,1)} %bitcast.19), calls=%async_computation.1 | async-start | bytes 524288 | tf_op jit(solution)/shard_map/all_to_all | solution.py:100
  151.1 125.4 %all-reduce.7.cloned.1.call-start = ((), (), s32[]{:S(2)}) async-start(), calls=%async_computation.10 | async-start | bytes 917504 | tf_op jit(solution)/shard_map/psum | solution.py:127
  151.2 4.6 %copy-start.8 = (bf16[1,1024,512]{1,2,0:T(8,128)(2,1)S(1)}, bf16[1,1024,512]{1,2,0:T(8,128)(2,1)}, u32[]{:S(2)}) copy-start(bf16[1,1024,512]{1,2,0:T(8,128)(2,1)} %copy.51) | copy-start | bytes 3145732
  151.2 4.6 %copy-start.9 = (f32[1024,512]{0,1:T(8,128)S(1)}, f32[1024,512]{0,1:T(8,128)}, u32[]{:S(2)}) copy-start(f32[1024,512]{0,1:T(8,128)} %copy.63) | copy-start | bytes 6291460
  (9 other events, 9.7 us)
Sparse Core Ops, SparseCore 0:
  79.7 34.0 reduce-scatter.10
  116.1 30.7 reduce-scatter.6
  149.2 36.5 reduce-scatter.8
  188.0 40.2 reduce-scatter.4
  232.0 44.4 all-reduce.6
where the time goes:
time: 291 us; the launch traced here: 289 us
  local copies, waits for them, and re-layouts  70.7 us (24%)
  other arithmetic  69.9 us (24%)
  waiting for transfers between devices  63.8 us (22%)
  matrix products  30.4 us (10%)
  blocking collectives  27.4 us (9%)
  between operations  15.5 us (5%)
  starting transfers between devices  11.9 us (4%)
    reduce_scatter x1, waiting for transfers between devices, local(): lax.psum_scatter(partials[0], 'patch', scatter_dimension=0, tiled=True)  39.4 us
    dot_general x12, matrix products, product(): return jnp.dot(left, right, preferred_element_type=jnp.float32)  30.4 us
    unnamed x79, local copies, waits for them, and re-layouts  27.2 us
    psum x1, waiting for transfers between devices, local(): lax.psum(pieces[0].astype(jnp.bfloat16), 'group').astype(jnp.float32)  24.3 us
    unnamed x1, blocking collectives  17.2 us
    scatter-add x1, other arithmetic, local(): jax.ops.segment_sum(grad_input[:, 2 * features:], recv_index, num_segment...  10.3 us
    psum x1, blocking collectives, local(): lax.psum(pieces[2].astype(jnp.bfloat16), 'group').astype(jnp.float32)  10.2 us
    gather x2, local copies, waits for them, and re-layouts, local(): jnp.take(grad_joined[:, features:], recv_index, axis=0)  9.76 us
  transfers between devices with their start and end apart: 7, of which 2 were waited for; matrix products, arithmetic and copies ran while one was open for 37% of the time, Pallas kernels for 0%

commit v1 on v0

v1 whole, which is shorter than its diff:
```python
import functools

import jax
import jax.numpy as jnp
from jax import lax
from jax.experimental import pallas as pl
from jax.experimental.pallas import tpu as pltpu
from jax.sharding import PartitionSpec as P

epsilon = 1e-05
BF = jnp.bfloat16
F32 = jnp.float32
LANES = 128
PACK = 16
MESH = pl.DeviceIdType.MESH


def dot(left, right):
    return jnp.dot(left, right, preferred_element_type=F32)


def dot_rt(left, right):
    return lax.dot_general(left, right, (((1,), (1,)), ((), ())), preferred_element_type=F32)


def dot_lt(left, right):
    return lax.dot_general(left, right, (((0,), (0,)), ((), ())), preferred_element_type=F32)


def sigmoid(values):
    return 1.0 / (1.0 + jnp.exp(-values))


def silu_slope(values):
    squash = sigmoid(values)
    return squash * (1.0 + values * (1.0 - squash))


def normalize(values):
    centred = values - jnp.mean(values, axis=1, keepdims=True)
    inverse = lax.rsqrt(jnp.mean(centred * centred, axis=1, keepdims=True) + epsilon)
    return (centred * inverse, inverse)


def normalize_back(upstream, normed, inverse):
    return inverse * (
        upstream
        - jnp.mean(upstream, axis=1, keepdims=True)
        - normed * jnp.mean(upstream * normed, axis=1, keepdims=True)
    )


def hot(index, shape, axis, base):
    return jnp.where(lax.broadcasted_iota(jnp.int32, shape, axis) + base == index, 1.0, 0.0).astype(
        BF
    )


class Copies:
    def __init__(self, send_sems, recv_sems):
        self.send_sems, self.recv_sems, self.used = send_sems, recv_sems, 0

    def start(self, source, target, device):
        copy = pltpu.make_async_remote_copy(
            src_ref=source,
            dst_ref=target,
            send_sem=self.send_sems.at[self.used],
            recv_sem=self.recv_sems.at[self.used],
            device_id=device,
            device_id_type=MESH,
        )
        self.used += 1
        copy.start()
        return copy


def wait_all(copies):
    for copy in copies:
        copy.wait()


class Reduction:
    def __init__(self, copies, refs, depth, middle, place):
        self.copies, self.depth, self.middle = copies, depth, middle
        self.g, self.rc, self.a, self.r1x, self.r1y, self.b0, self.b1 = refs[:7]
        self.r2x, self.r2y, self.c, self.r3, self.f = refs[7:]
        self.gi, self.p, self.core, self.z, self.gx, self.gy, self.zs = place
        self.xpeer = {"group": self.gi + 1 - 2 * self.gx, "patch": self.p}
        self.ypeer = {"group": self.gi + 2 - 4 * self.gy, "patch": self.p}
        self.low = pl.ds(0, middle)
        self.high = pl.ds(middle, depth - middle)

    def step0(self):
        other = {"group": self.gi, "patch": self.p + 1 - 2 * self.core}
        self.wait = [self.copies.start(self.g.at[1 - self.core], self.rc, other)]

    def step1(self):
        wait_all(self.wait)

        @pl.loop(0, self.zs)
        def _(k):
            self.a[k] = (self.g[self.core, k].astype(F32) + self.rc[k].astype(F32)).astype(BF)

        self.wait = [
            self.copies.start(self.a.at[:, 1 - self.gx, :, self.low], self.r1x, self.xpeer),
            self.copies.start(self.a.at[:, :, 1 - self.gy, self.high], self.r1y, self.ypeer),
        ]

    def step2(self):
        wait_all(self.wait)

        @pl.loop(0, self.zs)
        def _(k):
            self.b0[k] = (
                self.a[k, self.gx, :, self.low].astype(F32) + self.r1x[k].astype(F32)
            ).astype(BF)
            self.b1[k] = (
                self.a[k, :, self.gy, self.high].astype(F32) + self.r1y[k].astype(F32)
            ).astype(BF)

        self.wait = [
            self.copies.start(self.b0.at[:, 1 - self.gy], self.r2y, self.ypeer),
            self.copies.start(self.b1.at[:, 1 - self.gx], self.r2x, self.xpeer),
        ]

    def step3(self):
        wait_all(self.wait)

        @pl.loop(0, self.zs)
        def _(k):
            self.c[k, self.low] = (
                self.b0[k, self.gy].astype(F32) + self.r2y[k].astype(F32)
            ).astype(BF)
            self.c[k, self.high] = (
                self.b1[k, self.gx].astype(F32) + self.r2x[k].astype(F32)
            ).astype(BF)

        self.wait = []
        for step in range(1, self.zs):
            there = lax.rem(self.z + step, self.zs)
            self.wait.append(
                self.copies.start(
                    self.c.at[there],
                    self.r3.at[step - 1],
                    {"group": self.gi, "patch": there * 2 + self.core},
                )
            )

    def step4(self):
        wait_all(self.wait)
        total = self.c[self.z].astype(F32)
        for step in range(1, self.zs):
            total += self.r3[step - 1].astype(F32)
        self.f[self.gx, self.gy] = total.astype(BF)
        low = self.f.at[self.gx, self.gy, self.low]
        high = self.f.at[self.gx, self.gy, self.high]
        self.wait = [
            self.copies.start(low, low, self.ypeer),
            self.copies.start(high, high, self.xpeer),
        ]

    def step5(self):
        wait_all(self.wait)
        low = self.f.at[self.gx, :, self.low]
        high = self.f.at[:, self.gy, self.high]
        self.wait = [
            self.copies.start(low, low, self.xpeer),
            self.copies.start(high, high, self.ypeer),
        ]

    def step6(self, outs, factor):
        wait_all(self.wait)
        for quarter in range(4):
            row = 0
            for out in outs:
                size = out.shape[0]
                out[:, quarter * LANES : (quarter + 1) * LANES] = (
                    self.f[quarter // 2, quarter % 2, row : row + size].astype(F32) * factor
                )
                row += size


def kernel(sizes, *refs):
    n_group, n_patch, padded, tile, tile_edges, fused, factor = sizes
    (
        node,
        edge,
        node_cot,
        edge_cot,
        w_ei,
        w_eo,
        gain_e,
        w_ni,
        w_no,
        gain_n,
        send_col,
        send_row,
        recv_col,
        recv_row,
        list_col,
        list_row,
        count,
    ) = refs[:17]
    edge_grad, node_grad, o_ei, o_eo, o_ni, o_no, o_gain = refs[17:24]
    (
        outgoing,
        incoming,
        spread,
        returned,
        x_s,
        x_r,
        e_first,
        hidden,
        normed,
        inverse,
        message,
        joined,
        n_hidden,
        g_second,
        g_first,
        acc,
        gj,
        ge_second,
        ge_first,
        gs,
        gr,
        gains,
        send_sems,
        recv_sems,
    ) = refs[24:48]
    nodes, width = node.shape
    edges = edge.shape[0]
    halo = n_patch * padded
    gi = lax.axis_index("group")
    p = lax.axis_index("patch")
    core = lax.rem(p, 2)
    z = lax.div(p, 2)
    gx = lax.rem(gi, 2)
    gy = lax.div(gi, 2)
    copies = Copies(send_sems, recv_sems)

    barrier = pltpu.get_barrier_semaphore()
    peers = [{"group": gi, "patch": lax.rem(p + d, n_patch)} for d in range(1, n_patch)]
    greeted = list(peers)
    if fused:
        greeted.append({"group": gi + 1 - 2 * gx, "patch": p})
        greeted.append({"group": gi + 2 - 4 * gy, "patch": p})
    for peer in greeted:
        pl.semaphore_signal(barrier, inc=1, device_id=peer, device_id_type=MESH)

    chosen = dot(hot(list_col[...], (halo, nodes), 1, 0), node[...]).astype(BF)
    outgoing[...] = chosen.reshape(n_patch, padded, width)
    pl.semaphore_wait(barrier, len(greeted))
    moving = [
        copies.start(outgoing.at[lax.rem(p + d, n_patch)], incoming.at[p], peers[d - 1])
        for d in range(1, n_patch)
    ]
    incoming[p] = outgoing[p]
    gains[...] = jnp.zeros_like(gains)

    def rows_of(k):
        return pl.ds(pl.multiple_of(k * tile, tile), tile)

    @pl.loop(0, edges // tile)
    def _(k):
        rows = rows_of(k)
        latent = dot(hot(recv_col[rows, :], (tile, nodes), 1, 0), node[...]).astype(BF)
        x_r[rows, :] = latent
        e_first[rows, :] = dot(edge[rows, :], w_ei[:width, :]) + dot(latent, w_ei[2 * width :, :])

    wait_all(moving)

    def live_of(k):
        slot = lax.broadcasted_iota(jnp.int32, (tile, 1), 0) + k * tile
        return jnp.where(slot < count[0] * tile_edges, 1.0, 0.0)

    @pl.loop(0, edges // tile)
    def _(k):
        rows = rows_of(k)
        index = send_col[rows, :]
        latent = dot(hot(index, (tile, nodes), 1, 0), node[...])
        latent += dot(hot(index, (tile, halo), 1, nodes), incoming[...].reshape(halo, width))
        latent = latent.astype(BF)
        x_s[rows, :] = latent
        first = e_first[rows, :] + dot(latent, w_ei[width : 2 * width, :])
        e_first[rows, :] = first
        hid = (first * sigmoid(first)).astype(BF)
        hidden[rows, :] = hid
        norm, inv = normalize(dot(hid, w_eo[...]))
        normed[rows, :] = norm
        inverse[rows, :] = inv
        message[rows, :] = (live_of(k) * (gain_e[...] * norm)).astype(BF)

    @pl.loop(0, nodes // tile)
    def _(k):
        rows = rows_of(k)
        got = dot(hot(recv_row[...], (tile, edges), 0, k * tile), message[...]).astype(BF)
        joined[rows, :] = got
        first = dot(node[rows, :], w_ni[:width, :]) + dot(got, w_ni[width:, :])
        hid = (first * sigmoid(first)).astype(BF)
        n_hidden[rows, :] = hid
        norm, inv = normalize(dot(hid, w_no[...]))
        up = node_cot[rows, :].astype(F32)
        gains[1:2, :] += jnp.sum(up * norm, axis=0, keepdims=True)
        second = normalize_back(up * gain_n[...], norm, inv).astype(BF)
        g_second[rows, :] = second
        grad = (dot_rt(second, w_no[...]) * silu_slope(first)).astype(BF)
        g_first[rows, :] = grad
        acc[rows, :] = up + dot_rt(grad, w_ni[:width, :])
        gj[rows, :] = dot_rt(grad, w_ni[width:, :]).astype(BF)

    if fused:
        red_n_refs, red_e_refs = refs[48:60], refs[60:72]
        zs = n_patch // 2
        place = (gi, p, core, z, gx, gy, zs)
        g_n, g_e = red_n_refs[0], red_e_refs[0]
        red_n = Reduction(copies, red_n_refs, g_n.shape[-2], red_n_refs[3].shape[-2], place)
        red_e = Reduction(copies, red_e_refs, g_e.shape[-2], red_e_refs[3].shape[-2], place)

        def put(target, k, row, size, value):
            value = value.astype(BF)
            for c in range(2):
                for quarter in range(4):
                    target[c, k, quarter // 2, quarter % 2, row : row + size, :] = value[
                        c * size : (c + 1) * size, quarter * LANES : (quarter + 1) * LANES
                    ]

        def terms(target, k, row, size, left, right, first=0):
            span = pl.ds(pl.multiple_of(k * 2 * size, LANES), 2 * size)
            put(target, k + first, row, size, dot_lt(left[:, span], right))

        d_ni, d_no = o_ni.shape[0], o_no.shape[0]
        d_ei, d_eo = o_ei.shape[0], o_eo.shape[0]
        half = zs // 2

        @pl.loop(0, half)
        def _(k):
            terms(g_n, k, 0, d_ni, node, g_first[...])
            terms(g_n, k, 0, d_ni, joined, g_first[...], half)

        @pl.loop(0, zs)
        def _(k):
            terms(g_n, k, d_ni, d_no, n_hidden, g_second[...])

        red_n.step0()
    else:
        o_ni[:width, :] = dot_lt(node[...], g_first[...])
        o_ni[width:, :] = dot_lt(joined[...], g_first[...])
        o_no[...] = dot_lt(n_hidden[...], g_second[...])

    def edge_back(k):
        rows = rows_of(k)
        taken = dot(hot(recv_col[rows, :], (tile, nodes), 1, 0), gj[...])
        live = live_of(k)
        norm = normed[rows, :]
        grad = live * (edge_cot[rows, :].astype(F32) + taken)
        gains[0:1, :] += jnp.sum(grad * norm, axis=0, keepdims=True)
        second = normalize_back(grad * gain_e[...], norm, inverse[rows, :]).astype(BF)
        ge_second[rows, :] = second
        ge_first[rows, :] = (
            dot_rt(second, w_eo[...]) * silu_slope(e_first[rows, :])
        ).astype(BF)

    count_tiles = edges // tile
    pl.loop(0, count_tiles // 2)(edge_back)
    if fused:
        red_n.step1()
    pl.loop(count_tiles // 2, count_tiles)(edge_back)

    if fused:
        red_n.step2()
        blocks = 2 * d_ei
        for k in range(zs):
            start, stop = k * blocks, (k + 1) * blocks
            parts = []
            for order, source in enumerate((edge, x_s, x_r)):
                lo = max(start, order * width) - order * width
                hi = min(stop, (order + 1) * width) - order * width
                if lo < hi:
                    parts.append(dot_lt(source[:, lo:hi], ge_first[...]))
            value = parts[0] if len(parts) == 1 else jnp.concatenate(parts, axis=0)
            put(g_e, k, 0, d_ei, value)

        @pl.loop(0, zs)
        def _(k):
            terms(g_e, k, d_ei, d_eo, hidden, ge_second[...])
            total = gains[...]
            put(g_e, k, d_ei + d_eo, PACK, jnp.concatenate([total, total], axis=0))

        red_e.step0()
        red_n.step3()
    else:
        o_ei[:width, :] = dot_lt(edge[...], ge_first[...])
        o_ei[width : 2 * width, :] = dot_lt(x_s[...], ge_first[...])
        o_ei[2 * width :, :] = dot_lt(x_r[...], ge_first[...])
        o_eo[...] = dot_lt(hidden[...], ge_second[...])
        o_gain[...] = gains[...]

    def input_back(k):
        rows = rows_of(k)
        grad = ge_first[rows, :]
        gs[rows, :] = dot_rt(grad, w_ei[width : 2 * width, :]).astype(BF)
        gr[rows, :] = dot_rt(grad, w_ei[2 * width :, :]).astype(BF)

    pl.loop(0, count_tiles)(input_back)
    sums = dot(hot(send_row[...], (halo, edges), 0, nodes), gs[...]).astype(BF)
    spread[...] = sums.reshape(n_patch, padded, width)
    moving = [
        copies.start(spread.at[lax.rem(p + d, n_patch)], returned.at[p], peers[d - 1])
        for d in range(1, n_patch)
    ]
    returned[p] = spread[p]
    if fused:
        red_e.step1()
        red_n.step4()

    @pl.loop(0, count_tiles)
    def _(k):
        rows = rows_of(k)
        edge_grad[rows, :] = (
            live_of(k) * edge_cot[rows, :].astype(F32) + dot_rt(ge_first[rows, :], w_ei[:width, :])
        ).astype(BF)

    if fused:
        red_e.step2()
        red_n.step5()

    def gather_back(k):
        rows = rows_of(k)
        acc[rows, :] += dot(hot(send_row[...], (tile, edges), 0, k * tile), gs[...]) + dot(
            hot(recv_row[...], (tile, edges), 0, k * tile), gr[...]
        )

    pl.loop(0, nodes // tile)(gather_back)
    if fused:
        red_e.step3()
        red_n.step6((o_ni, o_no), factor)
    wait_all(moving)

    @pl.loop(0, nodes // tile)
    def _(k):
        rows = rows_of(k)
        node_grad[rows, :] = (
            acc[rows, :]
            + dot(
                hot(list_row[...], (tile, halo), 0, k * tile),
                returned[...].reshape(halo, width),
            )
        ).astype(BF)

    if fused:
        red_e.step4()
        red_e.step5()
        red_e.step6((o_ei, o_eo, o_gain), factor)


def reduction_scratch(zs, depth, middle):
    rest = depth - middle
    shapes = (
        (2, zs, 2, 2, depth),
        (zs, 2, 2, depth),
        (zs, 2, 2, depth),
        (zs, 2, middle),
        (zs, 2, rest),
        (zs, 2, middle),
        (zs, 2, rest),
        (zs, rest),
        (zs, middle),
        (zs, depth),
        (zs - 1, depth),
        (2, 2, depth),
    )
    return [pltpu.VMEM(shape + (LANES,), BF) for shape in shapes]


def local(
    n_group,
    n_patch,
    node_tape,
    edge_tape,
    node_cot,
    edge_cot,
    w_edge_in,
    w_edge_out,
    gain_edge,
    w_node_in,
    w_node_out,
    gain_node,
    senders,
    receivers,
    tile_count,
    send_rows,
):
    nodes, width = node_tape.shape[1:]
    edges = edge_tape.shape[1]
    listed = send_rows.shape[1]
    peer_rows = listed // n_patch
    padded = -(-peer_rows // PACK) * PACK
    halo = n_patch * padded
    tile = min(2 * LANES, nodes, edges)
    factor = float(n_group * n_patch * edges) ** (-0.5)

    flat = senders.reshape(-1)
    beyond = flat - nodes
    if padded != peer_rows:
        beyond = beyond // peer_rows * padded + beyond % peer_rows
        flat = jnp.where(flat < nodes, flat, nodes + beyond)
    lists = jnp.pad(
        send_rows.reshape(n_patch, peer_rows), ((0, 0), (0, padded - peer_rows)), constant_values=-1
    )
    recv = receivers.reshape(-1)

    weights = (w_edge_in, w_edge_out, w_node_in, w_node_out)
    depths = [w.shape[0] // n_patch for w in weights]
    zs = n_patch // 2
    fused = (
        n_group == 4
        and n_patch % 4 == 0
        and width == 4 * LANES
        and all(d % PACK == 0 and 2 * d % LANES == 0 for d in depths)
    )
    scratch = [
        pltpu.VMEM((n_patch, padded, width), BF),
        pltpu.VMEM((n_patch, padded, width), BF),
        pltpu.VMEM((n_patch, padded, width), BF),
        pltpu.VMEM((n_patch, padded, width), BF),
        pltpu.VMEM((edges, width), BF),
        pltpu.VMEM((edges, width), BF),
        pltpu.VMEM((edges, width), F32),
        pltpu.VMEM((edges, width), BF),
        pltpu.VMEM((edges, width), F32),
        pltpu.VMEM((edges, 1), F32),
        pltpu.VMEM((edges, width), BF),
        pltpu.VMEM((nodes, width), BF),
        pltpu.VMEM((nodes, width), BF),
        pltpu.VMEM((nodes, width), BF),
        pltpu.VMEM((nodes, width), BF),
        pltpu.VMEM((nodes, width), F32),
        pltpu.VMEM((nodes, width), BF),
        pltpu.VMEM((edges, width), BF),
        pltpu.VMEM((edges, width), BF),
        pltpu.VMEM((edges, width), BF),
        pltpu.VMEM((edges, width), BF),
        pltpu.VMEM((PACK, width), F32),
    ]
    n_copies = 2 * (n_patch - 1)
    if fused:
        d_ei, d_eo, d_ni, d_no = depths
        depth_n = d_ni + d_no
        depth_e = d_ei + d_eo + PACK
        scratch_n = reduction_scratch(zs, depth_n, depth_n // 2 // PACK * PACK)
        scratch_e = reduction_scratch(zs, depth_e, -(-depth_e // 2 // PACK) * PACK)
        n_copies += 2 * (9 + zs - 1)
    else:
        d_ei, d_eo, d_ni, d_no = [w.shape[0] for w in weights]
        scratch_n, scratch_e = [], []
    scratch += [pltpu.SemaphoreType.DMA((n_copies,)), pltpu.SemaphoreType.DMA((n_copies,))]
    scratch += scratch_n + scratch_e

    vmem = pl.BlockSpec(memory_space=pltpu.VMEM)
    sizes = (n_group, n_patch, padded, tile, senders.shape[1], fused, factor)
    edge_grad, node_grad, p_ei, p_eo, p_ni, p_no, p_gain = pl.pallas_call(
        functools.partial(kernel, sizes),
        out_shape=[
            jax.ShapeDtypeStruct((edges, width), BF),
            jax.ShapeDtypeStruct((nodes, width), BF),
            jax.ShapeDtypeStruct((d_ei, width), F32),
            jax.ShapeDtypeStruct((d_eo, width), F32),
            jax.ShapeDtypeStruct((d_ni, width), F32),
            jax.ShapeDtypeStruct((d_no, width), F32),
            jax.ShapeDtypeStruct((PACK, width), F32),
        ],
        in_specs=[vmem] * 16 + [pl.BlockSpec(memory_space=pltpu.SMEM)],
        out_specs=[vmem] * 7,
        scratch_shapes=scratch,
        compiler_params=pltpu.CompilerParams(
            collective_id=0, has_side_effects=True, vmem_limit_bytes=63 * 1024 * 1024
        ),
    )(
        node_tape[0],
        edge_tape[0],
        node_cot[0],
        edge_cot[0],
        w_edge_in,
        w_edge_out,
        gain_edge[None],
        w_node_in,
        w_node_out,
        gain_node[None],
        flat[:, None],
        flat[None],
        recv[:, None],
        recv[None],
        lists.reshape(-1, 1),
        lists.reshape(1, -1),
        tile_count,
    )
    piece = width // n_patch
    if fused:
        own = lax.dynamic_slice(p_gain, (0, lax.axis_index("patch") * piece), (2, piece))
        return (edge_grad[None], node_grad[None], p_ei, p_eo, own[0], p_ni, p_no, own[1])

    def summed(value):
        part = lax.psum_scatter(value, "patch", scatter_dimension=0, tiled=True)
        return lax.psum(part.astype(BF), "group").astype(F32) * factor

    return (
        edge_grad[None],
        node_grad[None],
        summed(p_ei),
        summed(p_eo),
        summed(p_gain[0]),
        summed(p_ni),
        summed(p_no),
        summed(p_gain[1]),
    )


def solution(mesh):
    member = P("group", "patch", None)
    placed = (member,) * 4 + (P(),) * 6
    placed += (P("patch", None), P("patch", None), P("patch"), P("patch", None))
    rows = P("patch", None)
    return jax.shard_map(
        functools.partial(local, mesh.shape["group"], mesh.shape["patch"]),
        mesh=mesh,
        in_specs=placed,
        out_specs=(member, member, rows, rows, P("patch"), rows, rows, P("patch")),
        check_vma=False,
    )
```

time: 291 us -> 87.9 us (0.30)
  Pallas kernels: 0 us -> 73.9 us
  other arithmetic: 69.9 us -> 0 us
  waiting for transfers between devices: 63.8 us -> 0 us
  local copies, waits for them, and re-layouts: 70.7 us -> 12.4 us
  matrix products: 30.4 us -> 0 us
  blocking collectives: 27.4 us -> 0 us
  between operations: 15.5 us -> 1.32 us
  starting transfers between devices: 11.9 us -> 0 us
    pallas_call x0 -> x1, Pallas kernels: none -> 73.9 us  [local(): pl.pallas_call(functools.partial(kernel, sizes), out_shape=[jax.ShapeDtyp...]
    reduce_scatter x4 -> x0, waiting for transfers between devices: 39.4 us -> none  [the longest x1 39.4 us: local(): lax.psum_scatter(partials[0], 'patch', scatter_dimension=0, tiled=True)]
    scatter-add x4 -> x0, other arithmetic: 31.6 us -> none  [the longest x1 10.3 us: local(): jax.ops.segment_sum(grad_input[:, 2 * features:], recv_index, num_segment...]
    dot_general x12 -> x0, matrix products: 30.4 us -> none  [product(): return jnp.dot(left, right, preferred_element_type=jnp.float32)]
    gather x7 -> x0, local copies, waits for them, and re-layouts: 28.5 us -> none  [the longest x2 9.76 us: local(): jnp.take(grad_joined[:, features:], recv_index, axis=0)]
    psum x1 -> x0, waiting for transfers between devices: 24.3 us -> none  [local(): lax.psum(pieces[0].astype(jnp.bfloat16), 'group').astype(jnp.float32)]
    unnamed x79 -> x16, local copies, waits for them, and re-layouts: 27.2 us -> 6.2 us
    unnamed x1 -> x0, blocking collectives: 17.2 us -> none
  transfers between devices with their start and end apart: 7 -> 0, of which waited for: 2 -> 0; matrix products, arithmetic and copies ran while one was open for 37% -> 0% of each run, Pallas kernels for 0% -> 0%
where the time goes in v1:
time: 87.9 us; the launch traced here: 87.6 us
  Pallas kernels  73.9 us (84%)
  local copies, waits for them, and re-layouts  12.4 us (14%)
  between operations  1.32 us (2%)
    pallas_call x1, Pallas kernels, local(): pl.pallas_call(functools.partial(kernel, sizes), out_shape=[jax.ShapeDtyp...  73.9 us
    unnamed x16, local copies, waits for them, and re-layouts  6.2 us

profile of v1, /device:TPU:0, one launch (start us, length us, event | category | flops | bytes accessed | tf_op | source)
XLA Modules:
  0.0 87.6 jit_solution(15890561974640460454)
XLA Ops:
  0.6 1.7 %copy.22.refs_10_ = s32[1024,1]{1,0:T(8,128)} copy(s32[1024,1]{0,1:T(1,128)} %bitcast.23) | data formatting | bytes 8192 | tf_op jit(solution)/shard_map/broadcast_in_dim;reshape | solution.py:590
  2.3 1.7 %copy.23.refs_12_ = s32[1024,1]{1,0:T(8,128)} copy(s32[1024,1]{0,1:T(1,128)} %bitcast.25) | data formatting | bytes 8192 | tf_op jit(solution)/shard_map/broadcast_in_dim;reshape | solution.py:592
  4.0 1.5 %copy.24.refs_14_ = s32[256,1]{1,0:T(8,128)} copy(s32[256,1]{0,1:T(1,128)} %bitcast.27) | data formatting | bytes 2048 | tf_op jit(solution)/shard_map/reshape | solution.py:594
  6.2 73.9 %shard_map.197 = (bf16[1024,512]{1,0:T(8,128)(2,1)}, bf16[1024,512]{1,0:T(8,128)(2,1)}, f32[192,512]{1,0:T(8,128)}, f32[64,512]{1,0:T(8,128)}, f32[128,512]{1,0:...) custom-call(bf16[1024,512]{1,0:T(8,128)(2,1)} %bitcast.19, bf16[1024,512]{1,0:T(8,128)(2,1)} %bitcast.20, ...), custom_call_target="tpu_custom_call" | custom-call | tf_op jit(solution)/shard_map/pallas_call | solution.py:562
  80.1 0.0 copy-start
  80.1 0.8 constant_dynamic-slice_fusion
  80.9 0.5 slice_bitcast_fusion
  81.4 2.3 %copy.32 = bf16[1,1024,512]{2,1,0:T(8,128)(2,1)} copy(bf16[1,1024,512]{2,1,0:T(8,128)(2,1)} %bitcast.18) | data formatting | bytes 2097152
  83.7 0.0 copy-done
  83.7 0.0 copy-start.1
  83.7 0.0 copy-start.4
  83.7 0.0 copy-start.2
  83.7 0.0 copy-start.3
  83.7 1.0 %copy.33 = bf16[1,1024,512]{2,1,0:T(8,128)(2,1)} copy(bf16[1,1024,512]{2,1,0:T(8,128)(2,1)S(1)} %bitcast.17) | data formatting | bytes 2097152
  84.7 0.2 copy-done.1
  84.9 0.7 copy.34
  85.6 0.0 copy-done.4
  85.6 0.7 copy.35
  86.3 0.0 copy-done.2
  86.3 0.7 copy.36
  87.0 0.0 copy-done.3
  87.0 0.7 copy.37
Async XLA Ops:
  80.1 3.6 %copy-start = (bf16[1024,512]{1,0:T(8,128)(2,1)S(1)}, bf16[1024,512]{1,0:T(8,128)(2,1)}, u32[]{:S(2)}) copy-start(bf16[1024,512]{1,0:T(8,128)(2,1)} %get-tuple-element.16) | copy-start | bytes 3145732
  83.7 1.2 %copy-start.1 = (f32[192,512]{1,0:T(8,128)S(1)}, f32[192,512]{1,0:T(8,128)}, u32[]{:S(2)}) copy-start(f32[192,512]{1,0:T(8,128)} %get-tuple-element.34) | copy-start | bytes 1179652
  83.7 1.9 %copy-start.4 = (f32[64,512]{1,0:T(8,128)S(1)}, f32[64,512]{1,0:T(8,128)}, u32[]{:S(2)}) copy-start(f32[64,512]{1,0:T(8,128)} %get-tuple-element.35) | copy-start | bytes 393220
  83.7 2.6 %copy-start.2 = (f32[128,512]{1,0:T(8,128)S(1)}, f32[128,512]{1,0:T(8,128)}, u32[]{:S(2)}) copy-start(f32[128,512]{1,0:T(8,128)} %get-tuple-element.37) | copy-start | bytes 786436
  83.7 3.3 %copy-start.3 = (f32[64,512]{1,0:T(8,128)S(1)}, f32[64,512]{1,0:T(8,128)}, u32[]{:S(2)}) copy-start(f32[64,512]{1,0:T(8,128)} %get-tuple-element.38) | copy-start | bytes 393220

commit v2 on v1

--- a/solution.py
+++ b/solution.py
@@ -182,26 +182,14 @@
 
 def kernel(sizes, *refs):
     n_group, n_patch, padded, tile, tile_edges, fused, factor = sizes
-    (
-        node,
-        edge,
-        node_cot,
-        edge_cot,
-        w_ei,
-        w_eo,
-        gain_e,
-        w_ni,
-        w_no,
-        gain_n,
-        send_col,
-        send_row,
-        recv_col,
-        recv_row,
-        list_col,
-        list_row,
-        count,
-    ) = refs[:17]
-    edge_grad, node_grad, o_ei, o_eo, o_ni, o_no, o_gain = refs[17:24]
+    stored = refs[:8]
+    gain_e, gain_n, send_tiles, recv_tiles, list_tiles, count = refs[8:14]
+    edge_out, node_out, o_ei, o_eo, o_ni, o_no, o_gain = refs[14:21]
+    loaded = refs[21:29]
+    node, edge, w_ei, w_eo, w_ni, w_no, node_cot, edge_cot = loaded
+    edge_grad, node_grad, load_sems, store_sems = refs[29:33]
+    send_col, send_row, recv_col, recv_row, list_col, list_row = refs[33:39]
+    refs = refs[15:]
     (
         outgoing,
         incoming,
@@ -238,6 +226,12 @@
     gx = lax.rem(gi, 2)
     gy = lax.div(gi, 2)
     copies = Copies(send_sems, recv_sems)
+    loads = [
+        pltpu.make_async_copy(source, target, load_sems.at[order])
+        for order, (source, target) in enumerate(zip(stored, loaded))
+    ]
+    for load in loads:
+        load.start()
 
     barrier = pltpu.get_barrier_semaphore()
     peers = [{"group": gi, "patch": lax.rem(p + d, n_patch)} for d in range(1, n_patch)]
@@ -248,6 +242,18 @@
     for peer in greeted:
         pl.semaphore_signal(barrier, inc=1, device_id=peer, device_id_type=MESH)
 
+    for tiles, column, line in (
+        (list_tiles, list_col, list_row),
+        (send_tiles, send_col, send_row),
+        (recv_tiles, recv_col, recv_row),
+    ):
+        turned = jnp.transpose(tiles[...].astype(F32)).astype(jnp.int32)
+        for order in range(line.shape[1] // LANES):
+            span = slice(order * LANES, (order + 1) * LANES)
+            column[span, :] = turned[:, order : order + 1]
+            line[:, span] = tiles[order : order + 1, :]
+
+    loads[0].wait()
     chosen = dot(hot(list_col[...], (halo, nodes), 1, 0), node[...]).astype(BF)
     outgoing[...] = chosen.reshape(n_patch, padded, width)
     pl.semaphore_wait(barrier, len(greeted))
@@ -258,6 +264,9 @@
     incoming[p] = outgoing[p]
     gains[...] = jnp.zeros_like(gains)
 
+    loads[1].wait()
+    loads[2].wait()
+
     def rows_of(k):
         return pl.ds(pl.multiple_of(k * tile, tile), tile)
 
@@ -268,6 +277,7 @@
         x_r[rows, :] = latent
         e_first[rows, :] = dot(edge[rows, :], w_ei[:width, :]) + dot(latent, w_ei[2 * width :, :])
 
+    loads[3].wait()
     wait_all(moving)
 
     def live_of(k):
@@ -290,6 +300,9 @@
         normed[rows, :] = norm
         inverse[rows, :] = inv
         message[rows, :] = (live_of(k) * (gain_e[...] * norm)).astype(BF)
+
+    for load in loads[4:]:
+        load.wait()
 
     @pl.loop(0, nodes // tile)
     def _(k):
@@ -310,12 +323,13 @@
         gj[rows, :] = dot_rt(grad, w_ni[width:, :]).astype(BF)
 
     if fused:
-        red_n_refs, red_e_refs = refs[48:60], refs[60:72]
+        red_n_refs, red_e_refs, red_o_refs = refs[48:60], refs[60:72], refs[72:84]
         zs = n_patch // 2
         place = (gi, p, core, z, gx, gy, zs)
-        g_n, g_e = red_n_refs[0], red_e_refs[0]
+        g_n, g_e, g_o = red_n_refs[0], red_e_refs[0], red_o_refs[0]
         red_n = Reduction(copies, red_n_refs, g_n.shape[-2], red_n_refs[3].shape[-2], place)
         red_e = Reduction(copies, red_e_refs, g_e.shape[-2], red_e_refs[3].shape[-2], place)
+        red_o = Reduction(copies, red_o_refs, g_o.shape[-2], red_o_refs[3].shape[-2], place)
 
         def put(target, k, row, size, value):
             value = value.astype(BF)
@@ -362,13 +376,10 @@
         ).astype(BF)
 
     count_tiles = edges // tile
-    pl.loop(0, count_tiles // 2)(edge_back)
+    pl.loop(0, count_tiles)(edge_back)
+
     if fused:
         red_n.step1()
-    pl.loop(count_tiles // 2, count_tiles)(edge_back)
-
-    if fused:
-        red_n.step2()
         blocks = 2 * d_ei
         for k in range(zs):
             start, stop = k * blocks, (k + 1) * blocks
@@ -381,14 +392,16 @@
             value = parts[0] if len(parts) == 1 else jnp.concatenate(parts, axis=0)
             put(g_e, k, 0, d_ei, value)
 
+        red_e.step0()
+        red_n.step2()
+
         @pl.loop(0, zs)
         def _(k):
-            terms(g_e, k, d_ei, d_eo, hidden, ge_second[...])
+            terms(g_o, k, 0, d_eo, hidden, ge_second[...])
             total = gains[...]
-            put(g_e, k, d_ei + d_eo, PACK, jnp.concatenate([total, total], axis=0))
-
-        red_e.step0()
-        red_n.step3()
+            put(g_o, k, d_eo, PACK, jnp.concatenate([total, total], axis=0))
+
+        red_o.step0()
     else:
         o_ei[:width, :] = dot_lt(edge[...], ge_first[...])
         o_ei[width : 2 * width, :] = dot_lt(x_s[...], ge_first[...])
@@ -412,7 +425,7 @@
     returned[p] = spread[p]
     if fused:
         red_e.step1()
-        red_n.step4()
+        red_n.step3()
 
     @pl.loop(0, count_tiles)
     def _(k):
@@ -421,9 +434,11 @@
             live_of(k) * edge_cot[rows, :].astype(F32) + dot_rt(ge_first[rows, :], w_ei[:width, :])
         ).astype(BF)
 
-    if fused:
-        red_e.step2()
-        red_n.step5()
+    stores = [pltpu.make_async_copy(edge_grad, edge_out, store_sems.at[0])]
+    stores[0].start()
+    if fused:
+        red_o.step1()
+        red_n.step4()
 
     def gather_back(k):
         rows = rows_of(k)
@@ -431,9 +446,16 @@
             hot(recv_row[...], (tile, edges), 0, k * tile), gr[...]
         )
 
-    pl.loop(0, nodes // tile)(gather_back)
+    middle = nodes // tile // 2
+    pl.loop(0, middle)(gather_back)
+    if fused:
+        red_e.step2()
+        red_o.step2()
+        red_n.step5()
+    pl.loop(middle, nodes // tile)(gather_back)
     if fused:
         red_e.step3()
+        red_o.step3()
         red_n.step6((o_ni, o_no), factor)
     wait_all(moving)
 
@@ -448,10 +470,25 @@
             )
         ).astype(BF)
 
+    stores.append(pltpu.make_async_copy(node_grad, node_out, store_sems.at[1]))
+    stores[1].start()
     if fused:
         red_e.step4()
+        red_o.step4()
         red_e.step5()
-        red_e.step6((o_ei, o_eo, o_gain), factor)
+        red_o.step5()
+        red_e.step6((o_ei,), factor)
+        red_o.step6((o_eo,), factor)
+        piece = o_gain.shape[1]
+        own = jnp.zeros(o_gain.shape, F32)
+        for quarter in range(4):
+            lane = lax.broadcasted_iota(jnp.int32, (LANES, piece), 0) + quarter * LANES
+            want = lax.broadcasted_iota(jnp.int32, (LANES, piece), 1) + p * piece
+            pick = jnp.where(lane == want, 1.0, 0.0).astype(BF)
+            own += dot(red_o.f[quarter // 2, quarter % 2, d_eo : d_eo + PACK], pick)
+        o_gain[...] = own * factor
+    for store in stores:
+        store.wait()
 
 
 def reduction_scratch(zs, depth, middle):
@@ -471,6 +508,12 @@
         (2, 2, depth),
     )
     return [pltpu.VMEM(shape + (LANES,), BF) for shape in shapes]
+
+
+def tiles_of(index):
+    rows = -(-index.shape[0] // LANES)
+    full = -(-rows // 8) * 8
+    return jnp.pad(index, (0, full * LANES - index.shape[0])).reshape(full, LANES)
 
 
 def local(
@@ -519,7 +562,19 @@
         and width == 4 * LANES
         and all(d % PACK == 0 and 2 * d % LANES == 0 for d in depths)
     )
-    scratch = [
+    own_rows = (node_tape[0], edge_tape[0], node_cot[0], edge_cot[0])
+    operands = own_rows[:2] + weights + own_rows[2:]
+    slots = -(-halo // LANES) * LANES
+    scratch = [pltpu.VMEM(operand.shape, BF) for operand in operands]
+    scratch += [
+        pltpu.VMEM((edges, width), BF),
+        pltpu.VMEM((nodes, width), BF),
+        pltpu.SemaphoreType.DMA((len(operands),)),
+        pltpu.SemaphoreType.DMA((2,)),
+    ]
+    for length in (edges, edges, slots):
+        scratch += [pltpu.VMEM((length, 1), jnp.int32), pltpu.VMEM((1, length), jnp.int32)]
+    scratch += [
         pltpu.VMEM((n_patch, padded, width), BF),
         pltpu.VMEM((n_patch, padded, width), BF),
         pltpu.VMEM((n_patch, padded, width), BF),
@@ -547,17 +602,21 @@
     if fused:
         d_ei, d_eo, d_ni, d_no = depths
         depth_n = d_ni + d_no
-        depth_e = d_ei + d_eo + PACK
+        depth_o = d_eo + PACK
+        piece = width // n_patch
         scratch_n = reduction_scratch(zs, depth_n, depth_n // 2 // PACK * PACK)
-        scratch_e = reduction_scratch(zs, depth_e, -(-depth_e // 2 // PACK) * PACK)
-        n_copies += 2 * (9 + zs - 1)
+        scratch_e = reduction_scratch(zs, d_ei, d_ei // 2 // PACK * PACK)
+        scratch_e += reduction_scratch(zs, depth_o, depth_o // 2 // PACK * PACK)
+        n_copies += 3 * (9 + zs - 1)
     else:
         d_ei, d_eo, d_ni, d_no = [w.shape[0] for w in weights]
         scratch_n, scratch_e = [], []
+        piece = width
     scratch += [pltpu.SemaphoreType.DMA((n_copies,)), pltpu.SemaphoreType.DMA((n_copies,))]
     scratch += scratch_n + scratch_e
 
     vmem = pl.BlockSpec(memory_space=pltpu.VMEM)
+    anywhere = pl.BlockSpec(memory_space=pl.ANY)
     sizes = (n_group, n_patch, padded, tile, senders.shape[1], fused, factor)
     edge_grad, node_grad, p_ei, p_eo, p_ni, p_no, p_gain = pl.pallas_call(
         functools.partial(kernel, sizes),
@@ -568,37 +627,25 @@
             jax.ShapeDtypeStruct((d_eo, width), F32),
             jax.ShapeDtypeStruct((d_ni, width), F32),
             jax.ShapeDtypeStruct((d_no, width), F32),
-            jax.ShapeDtypeStruct((PACK, width), F32),
+            jax.ShapeDtypeStruct((PACK, piece), F32),
         ],
-        in_specs=[vmem] * 16 + [pl.BlockSpec(memory_space=pltpu.SMEM)],
-        out_specs=[vmem] * 7,
+        in_specs=[anywhere] * 8 + [vmem] * 5 + [pl.BlockSpec(memory_space=pltpu.SMEM)],
+        out_specs=[anywhere] * 2 + [vmem] * 5,
         scratch_shapes=scratch,
         compiler_params=pltpu.CompilerParams(
             collective_id=0, has_side_effects=True, vmem_limit_bytes=63 * 1024 * 1024
         ),
     )(
-        node_tape[0],
-        edge_tape[0],
-        node_cot[0],
-        edge_cot[0],
-        w_edge_in,
-        w_edge_out,
+        *operands,
         gain_edge[None],
-        w_node_in,
-        w_node_out,
         gain_node[None],
-        flat[:, None],
-        flat[None],
-        recv[:, None],
-        recv[None],
-        lists.reshape(-1, 1),
-        lists.reshape(1, -1),
+        tiles_of(flat),
+        tiles_of(recv),
+        tiles_of(lists.reshape(-1)),
         tile_count,
     )
-    piece = width // n_patch
-    if fused:
-        own = lax.dynamic_slice(p_gain, (0, lax.axis_index("patch") * piece), (2, piece))
-        return (edge_grad[None], node_grad[None], p_ei, p_eo, own[0], p_ni, p_no, own[1])
+    if fused:
+        return (edge_grad[None], node_grad[None], p_ei, p_eo, p_gain[0], p_ni, p_no, p_gain[1])
 
     def summed(value):
         part = lax.psum_scatter(value, "patch", scatter_dimension=0, tiled=True)

time: 87.9 us -> 83.9 us (0.954)
  local copies, waits for them, and re-layouts: 12.4 us -> 8.62 us
    another operation x2 -> x0, local copies, waits for them, and re-layouts: 3.41 us -> none  [the longest x1 1.71 us: local(): flat[:, None]]
where the time goes in v2:
time: 83.9 us; the launch traced here: 83.6 us
  Pallas kernels  73.7 us (88%)
  local copies, waits for them, and re-layouts  8.62 us (10%)
  between operations  1.31 us (2%)
    pallas_call x1, Pallas kernels, local(): pl.pallas_call(functools.partial(kernel, sizes), out_shape=[jax.ShapeDtyp...  73.7 us
    unnamed x16, local copies, waits for them, and re-layouts  6.06 us

profile of v2, /device:TPU:0, one launch (start us, length us, event | category | flops | bytes accessed | tf_op | source)
XLA Modules:
  0.0 83.6 jit_solution(13014725849271418350)
XLA Ops:
  0.6 1.3 %pad_bitcast_fusion.refs_12_ = s32[8,128]{1,0:T(8,128)} fusion(s32[256]{0:T(256)} %bitcast.23), kind=kLoop, calls=%fused_computation | loop fusion | bytes 5120 | tf_op jit(solution)/shard_map/reshape | solution.py:516
  2.6 73.7 %shard_map.197 = (bf16[1024,512]{1,0:T(8,128)(2,1)}, bf16[1024,512]{1,0:T(8,128)(2,1)}, f32[192,512]{1,0:T(8,128)}, f32[64,512]{1,0:T(8,128)}, f32[128,512]{1,0:...) custom-call(bf16[1024,512]{1,0:T(8,128)(2,1)} %bitcast.15, bf16[1024,512]{1,0:T(8,128)(2,1)} %bitcast.16, ...), custom_call_target="tpu_custom_call" | custom-call | tf_op jit(solution)/shard_map/pallas_call | solution.py:621
  76.2 0.0 copy-start
  76.2 1.3 %slice_bitcast_fusion = (f32[64]{0:T(128)}, f32[64]{0:T(128)}) fusion(f32[16,64]{1,0:T(8,128)} %get-tuple-element.19), kind=kLoop, calls=%fused_computation.1 | loop fusion | bytes 1024 | tf_op jit(solution)/shard_map/squeeze | solution.py:648
  77.5 0.0 copy-start.1
  77.5 2.3 %copy.29 = bf16[1,1024,512]{2,1,0:T(8,128)(2,1)} copy(bf16[1,1024,512]{2,1,0:T(8,128)(2,1)} %bitcast.20) | data formatting | bytes 2097152
  79.8 0.0 copy-done
  79.9 0.0 copy-start.4
  79.9 0.0 copy-start.2
  79.9 0.0 copy-start.3
  79.9 1.0 %copy.30 = bf16[1,1024,512]{2,1,0:T(8,128)(2,1)} copy(bf16[1,1024,512]{2,1,0:T(8,128)(2,1)S(1)} %bitcast.19) | data formatting | bytes 2097152
  80.8 0.0 copy-done.1
  80.8 0.7 copy.31
  81.6 0.0 copy-done.4
  81.6 0.7 copy.32
  82.2 0.0 copy-done.2
  82.2 0.7 copy.33
  82.9 0.0 copy-done.3
  82.9 0.7 copy.34
Async XLA Ops:
  76.2 3.6 %copy-start = (bf16[1024,512]{1,0:T(8,128)(2,1)S(1)}, bf16[1024,512]{1,0:T(8,128)(2,1)}, u32[]{:S(2)}) copy-start(bf16[1024,512]{1,0:T(8,128)(2,1)} %get-tuple-element.16) | copy-start | bytes 3145732
  77.5 3.3 %copy-start.1 = (f32[192,512]{1,0:T(8,128)S(1)}, f32[192,512]{1,0:T(8,128)}, u32[]{:S(2)}) copy-start(f32[192,512]{1,0:T(8,128)} %get-tuple-element.34) | copy-start | bytes 1179652
  79.9 1.7 %copy-start.4 = (f32[64,512]{1,0:T(8,128)S(1)}, f32[64,512]{1,0:T(8,128)}, u32[]{:S(2)}) copy-start(f32[64,512]{1,0:T(8,128)} %get-tuple-element.35) | copy-start | bytes 393220
  79.9 2.4 %copy-start.2 = (f32[128,512]{1,0:T(8,128)S(1)}, f32[128,512]{1,0:T(8,128)}, u32[]{:S(2)}) copy-start(f32[128,512]{1,0:T(8,128)} %get-tuple-element.37) | copy-start | bytes 786436
  79.9 3.1 %copy-start.3 = (f32[64,512]{1,0:T(8,128)S(1)}, f32[64,512]{1,0:T(8,128)}, u32[]{:S(2)}) copy-start(f32[64,512]{1,0:T(8,128)} %get-tuple-element.38) | copy-start | bytes 393220
